TPU v7x, 32 devices: a whole 2x2x4 slice. The times are simulated.
32 devices in a mesh: grp: 2 (over core), tp: 8 (over z, y), dp: 2 (over x).
Axes of the slice: x: 2, y: 2, z: 4, core: 2. Of those that a mesh axis runs over, the one named last changes fastest.
Arguments:
- base_inputs: bfloat16 [3, 128, 8192], P(None, 'dp', ('grp', 'tp')), may hold values from -6 to 6
- small_inputs: bfloat16 [2, 3, 128, 4096], P('grp', None, 'dp', 'tp'), may hold values from -6 to 6
- base_norm_gain: float32 [8192], replicated, may hold values from 0.1 to 1.9
- base_query: bfloat16 [8192, 8192], P(None, ('grp', 'tp')), may hold values from -0.0625 to 0.0625
- base_keys_values: bfloat16 [2, 8192, 1024], P(None, None, ('grp', 'tp')), may hold values from -0.0625 to 0.0625
- base_output: bfloat16 [8192, 8192], P(('grp', 'tp')), may hold values from -0.0625 to 0.0625
- base_cache: bfloat16 [2, 128, 1024, 128], P(None, 'dp', ('grp', 'tp')), may hold values from -600 to 600
- base_final_gain: float32 [8192], replicated, may hold values from 0.1 to 1.9
- base_unembed: bfloat16 [16384, 8192], P(('grp', 'tp')), may hold values from -20 to 20
- small_norm_gain: float32 [2, 4096], P('grp'), may hold values from 0.1 to 1.9
- small_projections: bfloat16 [2, 3, 4096, 4096], P('grp', None, None, 'tp'), may hold values from -0.09375 to 0.09375
- small_output: bfloat16 [2, 4096, 4096], P('grp', 'tp'), may hold values from -0.09375 to 0.09375
- small_cache: bfloat16 [2, 2, 128, 4096, 128], P('grp', None, 'dp', 'tp'), may hold values from -600 to 600
- small_final_gain: float32 [2, 4096], P('grp'), may hold values from 0.1 to 1.9
- small_unembed: bfloat16 [2, 2, 8192, 4096], P('grp', None, 'tp'), may hold values from -0.1875 to 0.1875
- lengths: int32 [128], P('dp'), may hold values from 1 to 128, as said below
- next_tokens: int32 [3, 128], P(None, 'dp'), may hold values from 0 to 16383
Outputs:
- log_probs: float32 [3, 128, 16384], P(None, 'dp', ('grp', 'tp'))
- chosen_total: float32 [128], P('dp')
Inputs may be any that keep to these rules, and one draw needn't show every extreme that they name: `lengths`: some row holds 128 cached positions.
All inputs are finite; a program needn't handle non-finite values.
Results may differ from a plain program's by a relative error of at most 0.0035.
Values may be sent and summed in bfloat16 or wider, within the bound.
A program may use at most 256 MiB of HBM per device.

v0:
```python
import math
import jax
import jax.numpy as jnp
from jax import lax
from jax.sharding import PartitionSpec as P

HD = 128
STEPS = 3
CACHE = 128
EPSILON = 1e-05
NEGATIVE = -1e30


def partner(array, axis, bit):
    return lax.ppermute(array, axis, [(i, i ^ 1 << bit) for i in range(lax.axis_size(axis))])


def rotate_pairs(values, positions, first_pair, head_size):
    pair_count = values.shape[-1] // 2
    pair_index = (first_pair + jnp.arange(pair_count)).astype(jnp.float32)
    frequency = jnp.exp(pair_index * (-2.0 * math.log(10000.0) / head_size))
    angles = positions.astype(jnp.float32)[:, None] * frequency[None, :]
    angles = angles.reshape((values.shape[0],) + (1,) * (values.ndim - 2) + (pair_count,))
    cosine = jnp.cos(angles)
    sine_part = jnp.sin(angles)
    paired = values.reshape(values.shape[:-1] + (pair_count, 2))
    even_part = paired[..., 0]
    odd_part = paired[..., 1]
    turned = jnp.stack(
        [even_part * cosine - odd_part * sine_part, even_part * sine_part + odd_part * cosine],
        axis=-1,
    )
    return turned.reshape(values.shape)


def norm_rows(values, gain_row):
    values = values.astype(jnp.float32)
    scaling = lax.rsqrt(jnp.mean(values * values, axis=-1, keepdims=True) + EPSILON)
    return (values * scaling * gain_row).astype(jnp.bfloat16)


def attention_weights(cached_scores, fresh_scores, visible, head_size):
    factor = 1.0 / math.sqrt(head_size)
    cached_scores = jnp.where(visible, cached_scores * factor, NEGATIVE)
    fresh_scores = fresh_scores * factor
    row_max = jnp.maximum(
        jnp.max(cached_scores, axis=-1, keepdims=True),
        jnp.max(fresh_scores, axis=-1, keepdims=True),
    )
    cached_exp = jnp.exp(cached_scores - row_max)
    fresh_exp = jnp.exp(fresh_scores - row_max)
    totals = jnp.sum(cached_exp, axis=-1, keepdims=True) + jnp.sum(
        fresh_exp, axis=-1, keepdims=True
    )
    return ((cached_exp / totals).astype(jnp.bfloat16), (fresh_exp / totals).astype(jnp.bfloat16))


def sum_slices(scores, share_count):
    for bit_index in range(share_count.bit_length() - 1):
        scores = scores + partner(scores, "tp", bit_index)
    return scores


def body(
    base_inputs,
    small_inputs,
    base_norm_gain,
    base_query,
    base_keys_values,
    base_output,
    base_cache,
    base_final_gain,
    base_unembed,
    small_norm_gain,
    small_projections,
    small_output,
    small_cache,
    small_final_gain,
    small_unembed,
    lengths,
    next_tokens,
):
    row_count = lengths.shape[0]
    slice_width = base_keys_values.shape[2]
    share_count = HD // slice_width
    group_size = base_query.shape[1] // slice_width
    slice_index = lax.axis_index("tp") % share_count
    first_pair = slice_index * (slice_width // 2)
    block_index = lax.axis_index(("grp", "tp"))
    vocab_width = base_unembed.shape[0]
    small_heads = small_projections.shape[3] // HD
    base_full = lax.all_gather(base_inputs, ("grp", "tp"), axis=2, tiled=True)
    small_full = lax.all_gather(small_inputs[0], "tp", axis=2, tiled=True)
    visible = (jnp.arange(CACHE)[None, :] < lengths[:, None])[:, None, :]
    base_keys_cache = base_cache[0]
    base_values_cache = base_cache[1]
    small_keys_cache = small_cache[0, 0].reshape(row_count, small_heads, HD, CACHE)
    small_values_cache = small_cache[0, 1].reshape(row_count, small_heads, HD, CACHE)
    small_table = small_unembed[0].reshape(-1, small_unembed.shape[3])
    base_new_keys = []
    base_new_values = []
    small_new_keys = []
    small_new_values = []
    log_steps = []
    chosen_total = jnp.zeros((row_count,), jnp.float32)
    for step_index in range(STEPS):
        positions = lengths + step_index
        small_normed = norm_rows(small_full[step_index], small_norm_gain[0])
        small_queries = jnp.dot(
            small_normed, small_projections[0, 0], preferred_element_type=jnp.float32
        ).reshape(row_count, small_heads, HD)
        small_queries = rotate_pairs(small_queries, positions, 0, HD).astype(jnp.bfloat16)
        small_key = jnp.dot(
            small_normed, small_projections[0, 1], preferred_element_type=jnp.float32
        ).reshape(row_count, small_heads, HD)
        small_new_keys.append(rotate_pairs(small_key, positions, 0, HD).astype(jnp.bfloat16))
        small_value = jnp.dot(
            small_normed, small_projections[0, 2], preferred_element_type=jnp.float32
        ).reshape(row_count, small_heads, HD)
        small_new_values.append(small_value.astype(jnp.bfloat16))
        small_fresh_keys = jnp.stack(small_new_keys, axis=-1)
        small_fresh_values = jnp.stack(small_new_values, axis=-1)
        small_cached_scores = jnp.einsum(
            "rhd,rhdl->rhl", small_queries, small_keys_cache, preferred_element_type=jnp.float32
        )
        small_fresh_scores = jnp.einsum(
            "rhd,rhdn->rhn", small_queries, small_fresh_keys, preferred_element_type=jnp.float32
        )
        small_cached_weights, small_fresh_weights = attention_weights(
            small_cached_scores, small_fresh_scores, visible, HD
        )
        small_head_values = jnp.einsum(
            "rhl,rhdl->rhd",
            small_cached_weights,
            small_values_cache,
            preferred_element_type=jnp.float32,
        )
        small_head_values = small_head_values + jnp.einsum(
            "rhn,rhdn->rhd",
            small_fresh_weights,
            small_fresh_values,
            preferred_element_type=jnp.float32,
        )
        small_head_values = small_head_values.astype(jnp.bfloat16).reshape(
            row_count, small_heads * HD
        )
        small_partial = jnp.dot(
            small_head_values, small_output[0], preferred_element_type=jnp.float32
        )
        small_mixed = lax.psum(small_partial, "tp")
        small_hidden = small_full[step_index].astype(jnp.float32) + small_mixed
        small_final = norm_rows(small_hidden, small_final_gain[0])
        small_logits = lax.dot_general(
            small_final, small_table, (((1,), (1,)), ((), ())), preferred_element_type=jnp.float32
        )
        small_logits = small_logits.reshape(row_count, 2, small_table.shape[0] // 2)
        paired_logits = lax.all_to_all(
            small_logits[None], "grp", split_axis=2, concat_axis=0, tiled=True
        )
        normed = norm_rows(base_full[step_index], base_norm_gain)
        queries = jnp.dot(normed, base_query, preferred_element_type=jnp.float32).reshape(
            row_count, group_size, slice_width
        )
        queries = rotate_pairs(queries, positions, first_pair, HD).astype(jnp.bfloat16)
        new_key = jnp.dot(normed, base_keys_values[0], preferred_element_type=jnp.float32)
        key_now = rotate_pairs(new_key, positions, first_pair, HD).astype(jnp.bfloat16)
        value_now = jnp.dot(normed, base_keys_values[1], preferred_element_type=jnp.float32).astype(
            jnp.bfloat16
        )
        base_new_keys.append(key_now)
        base_new_values.append(value_now)
        fresh_keys = jnp.stack(base_new_keys, axis=-1)
        fresh_values = jnp.stack(base_new_values, axis=-1)
        cached_scores = jnp.einsum(
            "rgd,rdl->rgl", queries, base_keys_cache, preferred_element_type=jnp.float32
        )
        fresh_scores = jnp.einsum(
            "rgd,rdn->rgn", queries, fresh_keys, preferred_element_type=jnp.float32
        )
        both_scores = sum_slices(
            jnp.concatenate([cached_scores, fresh_scores], axis=-1), share_count
        )
        cached_weights, fresh_weights = attention_weights(
            both_scores[..., :CACHE], both_scores[..., CACHE:], visible, HD
        )
        head_values = jnp.einsum(
            "rgl,rdl->rgd", cached_weights, base_values_cache, preferred_element_type=jnp.float32
        )
        head_values = head_values + jnp.einsum(
            "rgn,rdn->rgd", fresh_weights, fresh_values, preferred_element_type=jnp.float32
        )
        head_values = head_values.astype(jnp.bfloat16).reshape(row_count, group_size * slice_width)
        partial_value = jnp.dot(head_values, base_output, preferred_element_type=jnp.float32)
        mixed_sum = lax.psum(partial_value, ("grp", "tp"))
        hidden = base_full[step_index].astype(jnp.float32) + mixed_sum
        final_rows = norm_rows(hidden, base_final_gain)
        base_logits = lax.dot_general(
            final_rows, base_unembed, (((1,), (1,)), ((), ())), preferred_element_type=jnp.float32
        )
        steered = base_logits + paired_logits[0, :, 0] - paired_logits[1, :, 0]
        local_max = jnp.max(steered, axis=-1)
        token_local = next_tokens[step_index] - block_index * vocab_width
        token_hit = jnp.arange(vocab_width)[None, :] == token_local[:, None]
        picked_local = jnp.sum(jnp.where(token_hit, steered, 0.0), axis=-1)
        row_max = lax.pmax(local_max, ("grp", "tp"))
        exp_total, picked = lax.psum(
            (jnp.sum(jnp.exp(steered - row_max[:, None]), axis=-1), picked_local), ("grp", "tp")
        )
        log_norm = row_max + jnp.log(exp_total)
        log_steps.append(steered - log_norm[:, None])
        chosen_total = chosen_total + picked - log_norm
    return (jnp.stack(log_steps, axis=0), chosen_total)


def solution(mesh):
    placed = (
        P(None, "dp", ("grp", "tp")),
        P("grp", None, "dp", "tp"),
        P(),
        P(None, ("grp", "tp")),
        P(None, None, ("grp", "tp")),
        P(("grp", "tp"), None),
        P(None, "dp", ("grp", "tp"), None),
        P(),
        P(("grp", "tp"), None),
        P("grp", None),
        P("grp", None, None, "tp"),
        P("grp", "tp", None),
        P("grp", None, "dp", "tp", None),
        P("grp", None),
        P("grp", None, "tp", None),
        P("dp"),
        P(None, "dp"),
    )
    return jax.shard_map(
        body,
        mesh=mesh,
        in_specs=placed,
        out_specs=(P(None, "dp", ("grp", "tp")), P("dp")),
        check_vma=False,
    )
```

profile of v0, /device:TPU:0, one launch (start us, length us, event | category | flops | bytes accessed | tf_op | source)
XLA Modules:
  0.0 661.0 jit_solution(7503122877806506709)
XLA Ops:
  8.8 9.1 %slice_bitcast_fusion.1 = (bf16[512,4096]{0,1:T(8,128)(2,1)}, bf16[512,4096]{0,1:T(8,128)(2,1)}, bf16[512,4096]{0,1:T(8,128)(2,1)}) fusion(bf16[1,3,4096,512]{3,2,1,0:T(8,128)(2,1)} %param.27), kind=kLoop, calls=%fused_computation.19 | loop fusion | bytes 25165824 | tf_op jit(solution)/shard_map/dot_general | solution.py:113
  17.8 6.4 copy.294
  24.3 7.6 %dot_general.221 = bf16[4,64,2,4096]{3,2,1,0:T(2,128)(2,1)} reshape(bf16[512,4096]{1,0:T(8,128)(2,1)} %copy.294) | data formatting | bytes 8388608 | tf_op jit(solution)/shard_map/dot_general | solution.py:113
  31.9 6.4 copy.297
  38.4 6.5 copy.291
  44.8 7.6 %dot_general.217 = bf16[4,64,2,4096]{3,2,1,0:T(2,128)(2,1)} reshape(bf16[512,4096]{1,0:T(8,128)(2,1)} %copy.291) | data formatting | bytes 8388608 | tf_op jit(solution)/shard_map/dot_general | solution.py:109
  53.1 12.0 %fusion.262 = (bf16[1,1,64,512,128]{4,3,2,1,0:T(8,128)(2,1)}, bf16[1,1,64,512,128]{4,3,2,1,0:T(8,128)(2,1)}) fusion(bf16[1,2,64,512,128]{4,3,2,1,0:T(8,128)(2,1)} %param.29), kind=kLoop, calls=%fused_computation.419 | loop fusion | bytes 33554432 | tf_op jit(solution)/shard_map/slice | solution.py:97
  66.4 7.3 %fusion.28 = f32[64,4,64,2]{2,0,3,1:T(8,128)S(1)} fusion(bf16[4,64,2,4096]{3,2,1,0:T(2,128)(2,1)} %dot_general.217, f32[4096]{0:T(1024)S(1)} %bitcast.550, f32[64]{0:T(128)S(1)} %add_rsqrt_fusion.9, bf16[1,3,64,4096]{3,2,1,0:T(8,128)(2,1)} %all-gather.6.cloned.1.call-done), kind=kOutput, calls=%fused_computation.31 | convolution fusion | flops 269484032 | bytes 4866304 | tf_op jit(solution)/shard_map/dot_general | solution.py:109
  73.9 7.1 %fusion.22 = f32[64,4,64,2]{2,0,3,1:T(8,128)S(1)} fusion(bf16[4,64,2,4096]{3,2,1,0:T(2,128)(2,1)} %dot_general.221, f32[4096]{0:T(1024)S(1)} %bitcast.551, f32[64]{0:T(128)S(1)} %add_rsqrt_fusion.9, bf16[1,3,64,4096]{3,2,1,0:T(8,128)(2,1)S(1)} %copy-done.5), kind=kOutput, calls=%fused_computation.25 | convolution fusion | flops 269484032 | bytes 4866560 | tf_op jit(solution)/shard_map/dot_general | solution.py:113
  81.5 5.6 fusion.269
  87.6 19.6 %fusion.173 = f32[64,4,1,128]{3,2,1,0:T(1,128)S(1)} fusion(bf16[64,4,128,128]{3,2,1,0:T(8,128)(2,1)} %bitcast.520, bf16[64,4,128,1]{2,0,1,3:T(8,128)(2,1)S(1)} %fusion.197), kind=kOutput, calls=%fused_computation.254 | convolution fusion | flops 8388608 | bytes 8585216 | tf_op jit(solution)/shard_map/rhl,rhdl->rhd/dot_general | solution.py:132
  109.4 1.9 fusion.16
  112.0 11.4 %copy.275 = bf16[512,8192]{1,0:T(8,128)(2,1)} copy(bf16[512,8192]{0,1:T(8,128)(2,1)} %bitcast.528) | data formatting | bytes 16777216 | tf_op jit(solution)/shard_map/dot_general | solution.py:161
  123.3 14.1 %dot_general.201 = bf16[8,32,2,8192]{3,2,1,0:T(2,128)(2,1)} reshape(bf16[512,8192]{1,0:T(8,128)(2,1)} %copy.275) | data formatting | bytes 16777216 | tf_op jit(solution)/shard_map/dot_general | solution.py:161
  141.9 61.5 %all-reduce.8.cloned.1.call-done = f32[64,4096]{1,0:T(8,128)} async-done(((f32[64,4096]{1,0:T(8,128)}), f32[64,4096]{1,0:T(8,128)}) %all-reduce.8.cloned.1.call-update) | async-done | bytes 1048592 | tf_op jit(solution)/shard_map/psum | solution.py:150
  203.4 2.2 multiply_reduce_fusion.5
  205.6 7.2 %fusion.20 = f32[64,4,64,2]{2,0,3,1:T(8,128)S(1)} fusion(bf16[4,64,2,4096]{3,2,1,0:T(2,128)(2,1)} %dot_general.221, f32[64]{0:T(128)S(1)} %get-tuple-element.123, f32[4096]{0:T(1024)S(1)} %bitcast.553, bf16[1,3,64,4096]{3,2,1,0:T(8,128)(2,1)S(1)} %copy-done.5), kind=kOutput, calls=%fused_computation.23 | convolution fusion | flops 269484032 | bytes 4866560 | tf_op jit(solution)/shard_map/dot_general | solution.py:113
  212.9 5.1 fusion.26
  218.4 5.6 fusion.271
  224.7 7.2 %fusion.18 = f32[64,4,64,2]{2,0,3,1:T(8,128)S(1)} fusion(bf16[4,64,2,4096]{3,2,1,0:T(2,128)(2,1)} %dot_general.221, f32[64]{0:T(128)S(1)} %get-tuple-element.122, f32[4096]{0:T(1024)S(1)} %bitcast.555, bf16[1,3,64,4096]{3,2,1,0:T(8,128)(2,1)S(1)} %copy-done.5), kind=kOutput, calls=%fused_computation.21 | convolution fusion | flops 269484032 | bytes 4866560 | tf_op jit(solution)/shard_map/dot_general | solution.py:113
  232.0 5.1 fusion.24
  238.0 5.6 fusion.273
  244.7 3.7 fusion.66
  251.2 7.9 %fusion.169 = f32[64,4,1,128]{3,2,1,0:T(1,128)S(1)} fusion(bf16[64,4,128,128]{3,2,1,0:T(8,128)(2,1)} %bitcast.521, bf16[64,4,128,1]{2,0,1,3:T(8,128)(2,1)S(1)} %get-tuple-element.83), kind=kOutput, calls=%fused_computation.250 | convolution fusion | flops 8388608 | bytes 8585216 | tf_op jit(solution)/shard_map/rhl,rhdl->rhd/dot_general | solution.py:132
  259.6 4.4 fusion.171
  264.1 1.8 fusion.12
  265.9 1.8 fusion.14
  268.1 3.2 fusion.36
  271.9 9.5 %fusion.8 = f32[64,8,32,2]{0,2,3,1:T(8,128)S(1)} fusion(bf16[8,32,2,8192]{3,2,1,0:T(2,128)(2,1)} %dot_general.201, f32[64]{0:T(128)S(1)} %get-tuple-element.125, f32[8192]{0:T(1024)S(1)} %copy-done.49, bf16[3,64,8192]{2,1,0:T(8,128)(2,1)S(1)} %copy-done.4), kind=kOutput, calls=%fused_computation.8 | convolution fusion | flops 538968064 | bytes 9601536 | tf_op jit(solution)/shard_map/dot_general | solution.py:161
  281.8 2.3 fusion.88
  287.4 2.2 fusion.99
  293.9 1.9 pad_maximum_fusion.2
  295.8 2.3 copy.311
  300.1 9.4 %fusion.10 = f32[64,8,32,2]{0,2,3,1:T(8,128)S(1)} fusion(bf16[8,32,2,8192]{3,2,1,0:T(2,128)(2,1)} %dot_general.201, f32[8192]{0:T(1024)} %param.19, f32[64]{0:T(128)} %copy-done.52, bf16[3,64,8192]{2,1,0:T(8,128)(2,1)S(1)} %copy-done.4), kind=kOutput, calls=%fused_computation.10 | convolution fusion | flops 538968064 | bytes 9601280 | tf_op jit(solution)/shard_map/dot_general | solution.py:161
  313.2 1.9 pad_maximum_fusion.3
  315.1 2.2 copy.282
  318.0 9.0 %fusion.6 = f32[64,8,32,2]{0,2,3,1:T(8,128)S(1)} fusion(bf16[8,32,2,8192]{3,2,1,0:T(2,128)(2,1)} %dot_general.201, f32[64]{0:T(128)} %get-tuple-element.124, f32[8192]{0:T(1024)} %param.19, bf16[3,64,8192]{2,1,0:T(8,128)(2,1)S(1)} %copy-done.4), kind=kOutput, calls=%fused_computation.6 | convolution fusion | flops 538968064 | bytes 9601280 | tf_op jit(solution)/shard_map/dot_general | solution.py:161
  334.2 1.9 pad_maximum_fusion.1
  336.1 2.2 copy.333
  344.3 2.2 copy.283
  348.6 2.4 copy.312
  353.1 3.0 collective-permute-done.2
  356.1 2.2 copy.334
  364.7 2.6 fusion.94
  368.0 1.8 copy.288
  372.5 2.5 fusion.65
  378.5 1.9 fusion.96
  381.6 6.5 fusion.272
  388.1 6.5 fusion.268
  394.6 2.9 fusion.270
  398.2 13.1 %fusion.51 = f32[1,64,2,1024]{3,1,0,2:T(8,128)} fusion(bf16[1,2,1024,4096]{3,2,1,0:T(8,128)(2,1)} %param.31, f32[64,4096]{1,0:T(8,128)} %all-reduce.8.cloned.1.call-done, f32[4096]{0:T(1024)S(1)} %bitcast.559, f32[64]{0:T(128)S(1)} %copy-done.44, bf16[1,3,64,4096]{3,2,1,0:T(8,128)(2,1)} %all-gather.6.cloned.1.call-done), kind=kOutput, calls=%fused_computation.72 | convolution fusion | flops 1075052544 | bytes 18891008 | tf_op jit(solution)/shard_map/dot_general | solution.py:153
  411.2 2.3 multiply_reduce_fusion.4
  413.5 12.8 %fusion.57 = f32[1,64,2,1024]{3,1,0,2:T(8,128)} fusion(bf16[1,2,1024,4096]{3,2,1,0:T(8,128)(2,1)} %param.31, f32[64,4096]{1,0:T(8,128)} %get-tuple-element.38, f32[64]{0:T(128)S(1)} %add_rsqrt_fusion, f32[4096]{0:T(1024)S(1)} %bitcast.560, bf16[1,3,64,4096]{3,2,1,0:T(8,128)(2,1)} %all-gather.6.cloned.1.call-done), kind=kOutput, calls=%fused_computation.74 | convolution fusion | flops 1075052544 | bytes 18891008 | tf_op jit(solution)/shard_map/dot_general | solution.py:153
  426.4 4.2 all-to-all-start.2
  430.6 12.6 %fusion.54 = f32[1,64,2,1024]{3,1,0,2:T(8,128)} fusion(bf16[1,2,1024,4096]{3,2,1,0:T(8,128)(2,1)} %param.31, f32[64,4096]{1,0:T(8,128)} %get-tuple-element.39, f32[64]{0:T(128)S(1)} %add_rsqrt_fusion.4, f32[4096]{0:T(1024)S(1)} %bitcast.561, bf16[1,3,64,4096]{3,2,1,0:T(8,128)(2,1)} %all-gather.6.cloned.1.call-done), kind=kOutput, calls=%fused_computation.73 | convolution fusion | flops 1075052544 | bytes 18891008 | tf_op jit(solution)/shard_map/dot_general | solution.py:153
  443.2 92.3 %all-reduce.10.cloned.1.call-done = (f32[64,8192]{1,0:T(8,128)}, f32[64,8192]{1,0:T(8,128)}, f32[64,8192]{1,0:T(8,128)}) async-done(((f32[64,8192]{1,0:T(8,128)}, f32[64,8192]{1,0:T(8,128)}, f32[64,8192]{1,0:T(8,128)}), (f32[64,8192]{1,0:T(8,128)}, f32[64,8192]{1,0:T(8,128)}, f32[64,8192]{1,0:T(8,128)})) %all-reduce.10.cloned.1.call-update) | async-done | bytes 6291472 | tf_op jit(solution)/shard_map/psum | solution.py:194
  535.5 3.9 multiply_reduce_fusion.2
  539.4 4.2 all-to-all-start.1
  543.7 11.7 %fusion.265 = (f32[64]{0:T(128)S(1)}, f32[64,1024]{1,0:T(8,128)S(1)}) fusion(f32[2,1,64,1,1024]{4,2,3,1,0:T(8,128)} %bitcast.128, bf16[1024,8192]{1,0:T(8,128)(2,1)} %param.25, f32[64,8192]{1,0:T(8,128)} %get-tuple-element.32, f32[64]{0:T(128)S(1)} %add_rsqrt_fusion.2, f32[8192]{0:T(1024)S(1)} %copy-done.15, bf16[3,64,8192]{2,1,0:T(8,128)(2,1)S(1)} %copy-done.4), kind=kOutput, calls=%fused_computation.422 | convolution fusion | flops 1076559872 | bytes 20742912 | tf_op jit(solution)/shard_map/dot_general | solution.py:197
  555.4 4.5 all-to-all-start
  559.9 12.4 %fusion.266 = (f32[64]{0:T(128)S(1)}, f32[64,1024]{1,0:T(8,128)}) fusion(f32[2,1,64,1,1024]{4,2,3,1,0:T(8,128)} %bitcast.92, bf16[1024,8192]{1,0:T(8,128)(2,1)} %param.25, f32[64,8192]{1,0:T(8,128)} %get-tuple-element.34, f32[64]{0:T(128)S(1)} %add_rsqrt_fusion.6, f32[8192]{0:T(1024)S(1)} %copy-done.15, bf16[3,64,8192]{2,1,0:T(8,128)(2,1)S(1)} %copy-done.4), kind=kOutput, calls=%fused_computation.423 | convolution fusion | flops 1076559872 | bytes 20742912 | tf_op jit(solution)/shard_map/dot_general | solution.py:197
  572.4 12.5 %fusion.267 = (f32[64]{0:T(128)S(1)}, f32[64,1024]{1,0:T(8,128)}) fusion(f32[2,1,64,1,1024]{4,2,3,1,0:T(8,128)} %bitcast.52, bf16[1024,8192]{1,0:T(8,128)(2,1)} %param.25, f32[64,8192]{1,0:T(8,128)} %get-tuple-element.33, f32[8192]{0:T(1024)S(1)} %copy-done.15, f32[64]{0:T(128)S(1)} %add_rsqrt_fusion.10, bf16[3,64,8192]{2,1,0:T(8,128)(2,1)S(1)} %copy-done.4), kind=kOutput, calls=%fused_computation.424 | convolution fusion | flops 1076559872 | bytes 20742912 | tf_op jit(solution)/shard_map/dot_general | solution.py:197
  584.8 33.0 %all-reduce.2 = (f32[64]{0:T(128)S(1)}, f32[64]{0:T(128)S(1)}, f32[64]{0:T(128)S(1)}) all-reduce(f32[64]{0:T(128)S(1)} %get-tuple-element.116, f32[64]{0:T(128)S(1)} %get-tuple-element.118, f32[64]{0:T(128)S(1)} %get-tuple-element.120), channel_id=1, replica_groups=mesh['grp'=2,'tp'=8,'dp'=2] {'grp','tp'}, use_global_device_ids=true, to_apply=%region_47.48 | all-reduce | flops 192 | bytes 1536 | tf_op jit(solution)/shard_map/pmax | solution.py:205
  620.4 29.5 %all-reduce = (f32[64]{0:T(128)S(1)}, f32[64]{0:T(128)S(1)}, f32[64]{0:T(128)S(1)}, f32[64]{0:T(128)S(1)}, f32[64]{0:T(128)S(1)}, /*index=5*/f32[64]{0:T(128)S(1)}) all-reduce(f32[64]{0:T(128)S(1)} %get-tuple-element.18, f32[64]{0:T(128)S(1)} %get-tuple-element.16, ...), channel_id=1, replica_groups=mesh['grp'=2,'tp'=8,'dp'=2] {'grp','tp'}, use_global_device_ids=true, to_apply=%region_49.50 | all-reduce | flops 384 | bytes 3072 | tf_op jit(solution)/shard_map/psum | solution.py:206
  (291 shorter events, 70.6 us)
Async XLA Ops:
  8.0 57.1 %all-gather.6.cloned.1.call-start = ((), (), s32[]{:S(2)}) async-start(), calls=%async_computation.5 | async-start | bytes 1769472 | tf_op jit(solution)/shard_map/all_gather | solution.py:93
  8.7 194.6 %all-reduce.8.cloned.1.call-start = ((), (), s32[]{:S(2)}) async-start(), calls=%async_computation.4 | async-start | bytes 2097152 | tf_op jit(solution)/shard_map/psum | solution.py:150
  44.8 7.6 %copy-start.42 = (s32[64]{0:T(128)S(1)}, s32[64]{0:T(128)}, u32[]{:S(2)}) copy-start(s32[64]{0:T(128)} %param.32) | copy-start | bytes 772
  52.6 84.9 %copy-start.27 = (f32[64]{0:T(128)}, f32[64]{0:T(128)S(1)}, u32[]{:S(2)}) copy-start(f32[64]{0:T(128)S(1)} %get-tuple-element.109) | copy-start | bytes 772
  52.6 84.9 %copy-start.29 = (f32[64]{0:T(128)}, f32[64]{0:T(128)S(1)}, u32[]{:S(2)}) copy-start(f32[64]{0:T(128)S(1)} %get-tuple-element.110) | copy-start | bytes 772
  52.6 84.9 %copy-start.31 = (f32[64]{0:T(128)}, f32[64]{0:T(128)S(1)}, u32[]{:S(2)}) copy-start(f32[64]{0:T(128)S(1)} %get-tuple-element.111) | copy-start | bytes 772
  53.1 13.3 %copy-start.16 = (f32[1,4096]{1,0:T(1,128)S(1)}, f32[1,4096]{1,0:T(1,128)}, u32[]{:S(2)}) copy-start(f32[1,4096]{1,0:T(1,128)} %param.26) | copy-start | bytes 49156
  66.4 7.6 %copy-start.5 = (bf16[1,3,64,4096]{3,2,1,0:T(8,128)(2,1)S(1)}, bf16[1,3,64,4096]{3,2,1,0:T(8,128)(2,1)}, u32[]{:S(2)}) copy-start(bf16[1,3,64,4096]{3,2,1,0:T(8,128)(2,1)} %all-gather.6.cloned.1.call-done) | copy-start | bytes 4718596
  87.6 19.6 %copy-start = (bf16[512,4096]{1,0:T(8,128)(2,1)S(1)}, bf16[512,4096]{1,0:T(8,128)(2,1)}, u32[]{:S(2)}) copy-start(bf16[512,4096]{1,0:T(8,128)(2,1)} %copy.297) | copy-start | bytes 12582916
  107.2 2.2 copy-start.2
  111.3 156.8 %all-gather.4.cloned.1.call-start = ((), (), s32[]{:S(2)}) async-start(), calls=%async_computation.3 | async-start | bytes 3342336 | tf_op jit(solution)/shard_map/all_gather | solution.py:92
  111.9 299.3 %all-reduce.12.cloned.1.call-start = ((), (), s32[]{:S(2)}) async-start(), calls=%async_computation.7 | async-start | bytes 4194304 | tf_op jit(solution)/shard_map/psum | solution.py:150
  137.5 3.8 copy-start.43
  137.5 68.0 %copy-start.33 = (f32[32]{0:T(128)}, f32[32]{0:T(128)S(1)}, u32[]{:S(2)}) copy-start(f32[32]{0:T(128)S(1)} %multiply_exponential_fusion.1) | copy-start | bytes 388
  205.6 7.3 %copy-start.40 = (f32[64]{0:T(128)}, f32[64]{0:T(128)S(1)}, u32[]{:S(2)}) copy-start(f32[64]{0:T(128)S(1)} %get-tuple-element.123) | copy-start | bytes 772
  205.6 26.4 %copy-start.38 = (f32[64]{0:T(128)}, f32[64]{0:T(128)S(1)}, u32[]{:S(2)}) copy-start(f32[64]{0:T(128)S(1)} %get-tuple-element.122) | copy-start | bytes 772
  205.6 7.3 %copy-start.10 = (bf16[4,64,2,4096]{3,2,1,0:T(2,128)(2,1)S(1)}, bf16[4,64,2,4096]{3,2,1,0:T(2,128)(2,1)}, u32[]{:S(2)}) copy-start(bf16[4,64,2,4096]{3,2,1,0:T(2,128)(2,1)} %dot_general.217) | copy-start | bytes 12582916
  224.7 7.3 %copy-start.11 = (bf16[4,64,2,4096]{3,2,1,0:T(2,128)(2,1)S(1)}, bf16[4,64,2,4096]{3,2,1,0:T(2,128)(2,1)}, u32[]{:S(2)}) copy-start(bf16[4,64,2,4096]{3,2,1,0:T(2,128)(2,1)} %dot_general.217) | copy-start | bytes 12582916
  238.0 6.7 %copy-start.41 = (f32[64]{0:T(128)S(1)}, f32[64]{0:T(128)}, u32[]{:S(2)}) copy-start(f32[64]{0:T(128)} %copy-done.40) | copy-start | bytes 772
  243.7 4.8 copy-start.39
  244.7 3.8 copy-start.1
  248.4 1.5 copy-start.48
  248.5 11.1 %slice-start.2 = ((s8[8388608]{0:T(1024)(128)(4,1)}), s8[4194304]{0:T(1024)(128)(4,1)S(1)}, s32[]{:S(2)}) async-start(s8[8388608]{0:T(1024)(128)(4,1)} %bitcast.522), calls=%async_computation.10 | async-start | bytes 8388608
  251.2 8.4 %slice-start.3 = ((s8[8388608]{0:T(1024)(128)(4,1)}), s8[4194304]{0:T(1024)(128)(4,1)S(1)}, s32[]{:S(2)}) async-start(s8[8388608]{0:T(1024)(128)(4,1)} %bitcast.522), calls=%async_computation.11 | async-start | bytes 8388608
  259.6 4.5 copy-start.3
  267.8 4.2 copy-start.49
  267.8 267.7 %all-reduce.10.cloned.1.call-start = ((), (), s32[]{:S(2)}) async-start(), calls=%async_computation.6 | async-start | bytes 12582912 | tf_op jit(solution)/shard_map/psum | solution.py:194
  268.1 3.9 copy-start.4
  271.9 9.5 %copy-start.46 = (f32[64]{0:T(128)}, f32[64]{0:T(128)S(1)}, u32[]{:S(2)}) copy-start(f32[64]{0:T(128)S(1)} %get-tuple-element.125) | copy-start | bytes 772
  281.8 2.4 copy-start.12
  281.8 4.1 copy-start.30
  281.8 4.1 copy-start.32
  281.8 4.1 copy-start.34
  281.8 5.1 copy-start.45
  281.8 5.6 copy-start.50
  284.2 5.5 copy-start.28
  286.9 3.3 copy-start.25
  298.1 50.6 %collective-permute-start.1 = (f32[64,8,130]{2,1,0:T(8,128)}, f32[64,8,130]{2,1,0:T(8,128)}, u32[]{:S(2)}, u32[]{:S(2)}) collective-permute-start(f32[64,8,130]{2,1,0:T(8,128)} %copy.311), channel_id=1, source_target_pairs={{0,2},{2,0},{4,6},{6,4},{8,10},{10,8},{12,14},{14,12},{1,3},{3,1},... | collective-permute-start | bytes 798728 | tf_op jit(solution)/shard_map/ppermute | solution.py:15
  300.1 9.4 %copy-start.22 = (f32[64,32]{0,1:T(8,128)S(1)}, f32[64,32]{0,1:T(8,128)}, u32[]{:S(2)}) copy-start(f32[64,32]{0,1:T(8,128)} %get-tuple-element.95) | copy-start | bytes 24580
  300.1 9.4 %copy-start.23 = (f32[64,32]{0,1:T(8,128)S(1)}, f32[64,32]{0,1:T(8,128)}, u32[]{:S(2)}) copy-start(f32[64,32]{0,1:T(8,128)} %get-tuple-element.96) | copy-start | bytes 24580
  317.3 9.7 %copy-start.20 = (f32[64,32]{0,1:T(8,128)S(1)}, f32[64,32]{0,1:T(8,128)}, u32[]{:S(2)}) copy-start(f32[64,32]{0,1:T(8,128)} %get-tuple-element.107) | copy-start | bytes 24580
  317.3 9.8 %copy-start.21 = (f32[64,32]{0,1:T(8,128)S(1)}, f32[64,32]{0,1:T(8,128)}, u32[]{:S(2)}) copy-start(f32[64,32]{0,1:T(8,128)} %get-tuple-element.108) | copy-start | bytes 24580
  317.3 27.0 %collective-permute-start = (f32[64,8,129]{2,1,0:T(8,128)}, f32[64,8,129]{2,1,0:T(8,128)}, u32[]{:S(2)}, u32[]{:S(2)}) collective-permute-start(f32[64,8,129]{2,1,0:T(8,128)} %copy.282), channel_id=1, source_target_pairs={{0,2},{2,0},{4,6},{6,4},{8,10},{10,8},{12,14},{14,12},{1,3},{3,1},... | collective-permute-start | bytes 792584 | tf_op jit(solution)/shard_map/ppermute | solution.py:15
  333.1 8.3 %copy-start.51 = (f32[8192]{0:T(1024)S(1)}, f32[8192]{0:T(1024)}, u32[]{:S(2)}) copy-start(f32[8192]{0:T(1024)} %param.19) | copy-start | bytes 98308
  333.1 8.3 %copy-start.53 = (f32[64]{0:T(128)S(1)}, f32[64]{0:T(128)}, u32[]{:S(2)}) copy-start(f32[64]{0:T(128)} %copy-done.52) | copy-start | bytes 772
  338.3 3.1 copy-start.13
  338.3 4.3 copy-start.47
  338.3 17.8 %collective-permute-start.2 = (f32[64,8,131]{2,1,0:T(8,128)}, f32[64,8,131]{2,1,0:T(8,128)}, u32[]{:S(2)}, u32[]{:S(2)}) collective-permute-start(f32[64,8,131]{2,1,0:T(8,128)} %copy.333), channel_id=1, source_target_pairs={{0,2},{2,0},{4,6},{6,4},{8,10},{10,8},{12,14},{14,12},{1,3},{3,1},... | collective-permute-start | bytes 804872 | tf_op jit(solution)/shard_map/ppermute | solution.py:15
  342.6 4.0 copy-start.24
  342.6 8.5 %copy-start.19 = (f32[64,8,2]{0,1,2:T(8,128)S(1)}, f32[64,8,2]{0,1,2:T(8,128)}, u32[]{:S(2)}) copy-start(f32[64,8,2]{0,1,2:T(8,128)} %copy.310) | copy-start | bytes 12292
  347.8 0.8 copy-start.8
  352.3 0.8 copy-start.6
  358.3 2.9 copy-start.7
  358.3 3.3 copy-start.9
  381.6 6.5 copy-start.14
  381.6 13.0 %slice-start = ((s8[8388608]{0:T(1024)(128)(4,1)}), s8[4194304]{0:T(1024)(128)(4,1)S(1)}, s32[]{:S(2)}) async-start(s8[8388608]{0:T(1024)(128)(4,1)} %bitcast.518), calls=%async_computation.8 | async-start | bytes 8388608
  388.1 6.5 slice-start.1
  426.4 113.1 %all-to-all-start.2 = ((f32[1,64,2,1024]{3,1,0,2:T(8,128)}), f32[1,64,2,1024]{3,1,0,2:T(8,128)}, u32[]{:S(2)}, u32[]{:S(2)}) async-start(f32[1,64,2,1024]{3,1,0,2:T(8,128)} %fusion.57), calls=%async_computation.2 | async-start | bytes 1048576 | tf_op jit(solution)/shard_map/all_to_all | solution.py:157
  535.5 8.1 %copy-start.15 = (f32[8192]{0:T(1024)S(1)}, f32[8192]{0:T(1024)}, u32[]{:S(2)}) copy-start(f32[8192]{0:T(1024)} %param.24) | copy-start | bytes 98308
  539.4 16.0 %all-to-all-start.1 = ((f32[1,64,2,1024]{3,1,0,2:T(8,128)}), f32[1,64,2,1024]{3,1,0,2:T(8,128)}, u32[]{:S(2)}, u32[]{:S(2)}) async-start(f32[1,64,2,1024]{3,1,0,2:T(8,128)} %fusion.54), calls=%async_computation.1 | async-start | bytes 1048576 | tf_op jit(solution)/shard_map/all_to_all | solution.py:157
  555.4 16.9 %all-to-all-start = ((f32[1,64,2,1024]{3,1,0,2:T(8,128)}), f32[1,64,2,1024]{3,1,0,2:T(8,128)}, u32[]{:S(2)}, u32[]{:S(2)}) async-start(f32[1,64,2,1024]{3,1,0,2:T(8,128)} %fusion.51), calls=%async_computation | async-start | bytes 1048576 | tf_op jit(solution)/shard_map/all_to_all | solution.py:157
  572.3 45.5 %copy-start.37 = (s32[64]{0:T(128)S(1)}, s32[64]{0:T(128)}, u32[]{:S(2)}) copy-start(s32[64]{0:T(128)} %get-tuple-element.87) | copy-start | bytes 772
  572.3 45.7 %copy-start.36 = (s32[64]{0:T(128)S(1)}, s32[64]{0:T(128)}, u32[]{:S(2)}) copy-start(s32[64]{0:T(128)} %get-tuple-element.88) | copy-start | bytes 772
  572.3 46.9 %copy-start.35 = (s32[64]{0:T(128)S(1)}, s32[64]{0:T(128)}, u32[]{:S(2)}) copy-start(s32[64]{0:T(128)} %get-tuple-element.86) | copy-start | bytes 772
  (5 other events, 3.2 us)
Sparse Core Ops, SparseCore 0:
  10.8 47.1 all-gather.5
  111.4 91.8 all-reduce.7
  267.9 104.6 all-reduce.11
  397.6 137.8 all-reduce.9
Sparse Core Ops, SparseCore 1:
  113.9 52.9 all-gather.3
where the time goes:
time: 667 us; the launch traced here: 661 us
  matrix products  245 us (37%)
  waiting for transfers between devices  158 us (24%)
  local copies, waits for them, and re-layouts  118 us (18%)
  blocking collectives  62.5 us (9%)
  other arithmetic  43.7 us (7%)
  between operations  16.9 us (3%)
  starting transfers between devices  16.7 us (3%)
    psum x1, waiting for transfers between devices, body(): mixed_sum = lax.psum(partial_value, ('grp', 'tp'))  92.3 us
    psum x2, waiting for transfers between devices, body(): small_mixed = lax.psum(small_partial, 'tp')  61.5 us
    dot_general x3, matrix products, body(): lax.dot_general(small_final, small_table, (((1,), (1,)), ((), ())), prefe...  38.5 us
    dot_general x3, matrix products, body(): lax.dot_general(final_rows, base_unembed, (((1,), (1,)), ((), ())), prefe...  36.6 us
    pmax x1, blocking collectives, body(): row_max = lax.pmax(local_max, ('grp', 'tp'))  33 us
    dot_general x3, matrix products, body(): jnp.einsum('rhl,rhdl->rhd', small_cached_weights, small_values_cache, pre...  31.9 us
    psum x1, blocking collectives, body(): lax.psum((jnp.sum(jnp.exp(steered - row_max[:, None]), axis=-1), picked_l...  29.5 us
    dot_general x3, matrix products, body(): jnp.dot(normed, base_query, preferred_element_type=jnp.float32)  27.9 us
  transfers between devices with their start and end apart: 11, of which 3 were waited for; matrix products, arithmetic and copies ran while one was open for 51% of the time, Pallas kernels for 0%

commit v1 on v0

--- a/solution.py
+++ b/solution.py
@@ -191,7 +191,7 @@
         )
         head_values = head_values.astype(jnp.bfloat16).reshape(row_count, group_size * slice_width)
         partial_value = jnp.dot(head_values, base_output, preferred_element_type=jnp.float32)
-        mixed_sum = lax.psum(partial_value, ("grp", "tp"))
+        mixed_sum = lax.psum(lax.psum(partial_value, "tp"), "grp")
         hidden = base_full[step_index].astype(jnp.float32) + mixed_sum
         final_rows = norm_rows(hidden, base_final_gain)
         base_logits = lax.dot_general(

time: 667 us -> 853 us (1.28)
  waiting for transfers between devices: 158 us -> 340 us
    psum x1 -> x2, waiting for transfers between devices: 92.3 us -> 269 us  [body(): mixed_sum = lax.psum(lax.psum(partial_value, 'tp'), 'grp')]
    psum x2 -> x1, waiting for transfers between devices: 61.5 us -> 62.1 us  [body(): small_mixed = lax.psum(small_partial, 'tp')]
  transfers between devices with their start and end apart: 11 -> 11, of which waited for: 3 -> 4; matrix products, arithmetic and copies ran while one was open for 51% -> 30% of each run, Pallas kernels for 0% -> 0%
where the time goes in v1:
time: 853 us; the launch traced here: 847 us
  waiting for transfers between devices  340 us (40%)
  matrix products  248 us (29%)
  local copies, waits for them, and re-layouts  120 us (14%)
  blocking collectives  61.7 us (7%)
  other arithmetic  43.4 us (5%)
  between operations  16.8 us (2%)
  starting transfers between devices  16.6 us (2%)
    psum x2, waiting for transfers between devices, body(): mixed_sum = lax.psum(lax.psum(partial_value, 'tp'), 'grp')  269 us
    psum x1, waiting for transfers between devices, body(): small_mixed = lax.psum(small_partial, 'tp')  62.1 us
    dot_general x3, matrix products, body(): lax.dot_general(small_final, small_table, (((1,), (1,)), ((), ())), prefe...  40.7 us
    dot_general x3, matrix products, body(): lax.dot_general(final_rows, base_unembed, (((1,), (1,)), ((), ())), prefe...  36.6 us
    dot_general x3, matrix products, body(): jnp.einsum('rhl,rhdl->rhd', small_cached_weights, small_values_cache, pre...  31.9 us
    pmax x1, blocking collectives, body(): row_max = lax.pmax(local_max, ('grp', 'tp'))  30.9 us
    psum x1, blocking collectives, body(): lax.psum((jnp.sum(jnp.exp(steered - row_max[:, None]), axis=-1), picked_l...  30.8 us
    dot_general x3, matrix products, body(): jnp.dot(normed, base_query, preferred_element_type=jnp.float32)  27.2 us
  transfers between devices with their start and end apart: 11, of which 4 were waited for; matrix products, arithmetic and copies ran while one was open for 30% of the time, Pallas kernels for 0%

profile of v1, /device:TPU:0, one launch (start us, length us, event | category | flops | bytes accessed | tf_op | source)
XLA Modules:
  0.0 846.9 jit_solution(46878858176692123)
XLA Ops:
  8.8 9.0 %slice_bitcast_fusion.1 = (bf16[512,4096]{0,1:T(8,128)(2,1)}, bf16[512,4096]{0,1:T(8,128)(2,1)}, bf16[512,4096]{0,1:T(8,128)(2,1)}) fusion(bf16[1,3,4096,512]{3,2,1,0:T(8,128)(2,1)} %param.27), kind=kLoop, calls=%fused_computation.19 | loop fusion | bytes 25165824 | tf_op jit(solution)/shard_map/dot_general | solution.py:113
  17.8 6.4 copy.291
  24.2 7.6 dot_general.217
  31.8 6.4 copy.294
  38.2 7.6 dot_general.221
  46.0 6.4 copy.297
  53.4 12.0 %fusion.262 = (bf16[1,1,64,512,128]{4,3,2,1,0:T(8,128)(2,1)}, bf16[1,1,64,512,128]{4,3,2,1,0:T(8,128)(2,1)}) fusion(bf16[1,2,64,512,128]{4,3,2,1,0:T(8,128)(2,1)} %param.29), kind=kLoop, calls=%fused_computation.419 | loop fusion | bytes 33554432 | tf_op jit(solution)/shard_map/slice | solution.py:97
  66.7 7.3 fusion.28
  74.3 7.1 fusion.22
  81.8 5.6 fusion.269
  88.0 19.6 %fusion.173 = f32[64,4,1,128]{3,2,1,0:T(1,128)S(1)} fusion(bf16[64,4,128,128]{3,2,1,0:T(8,128)(2,1)} %bitcast.518, bf16[64,4,128,1]{2,0,1,3:T(8,128)(2,1)S(1)} %fusion.197), kind=kOutput, calls=%fused_computation.254 | convolution fusion | flops 8388608 | bytes 8585216 | tf_op jit(solution)/shard_map/rhl,rhdl->rhd/dot_general | solution.py:132
  109.8 1.9 fusion.16
  113.2 11.4 %copy.275 = bf16[512,8192]{1,0:T(8,128)(2,1)} copy(bf16[512,8192]{0,1:T(8,128)(2,1)} %bitcast.526) | data formatting | bytes 16777216 | tf_op jit(solution)/shard_map/dot_general | solution.py:161
  124.6 14.2 %dot_general.201 = bf16[8,32,2,8192]{3,2,1,0:T(2,128)(2,1)} reshape(bf16[512,8192]{1,0:T(8,128)(2,1)} %copy.275) | data formatting | bytes 16777216 | tf_op jit(solution)/shard_map/dot_general | solution.py:161
  141.7 62.1 %all-reduce.8.cloned.1.call-done = f32[64,4096]{1,0:T(8,128)} async-done(((f32[64,4096]{1,0:T(8,128)}), f32[64,4096]{1,0:T(8,128)}) %all-reduce.8.cloned.1.call-update) | async-done | bytes 1048592 | tf_op jit(solution)/shard_map/psum | solution.py:150
  203.7 2.3 multiply_reduce_fusion.5
  206.0 7.3 fusion.26
  213.2 5.1 fusion.20
  219.0 6.2 fusion.271
  225.2 5.1 fusion.24
  230.3 5.1 fusion.18
  236.1 5.6 fusion.273
  243.1 3.7 fusion.66
  249.0 7.9 fusion.171
  257.4 4.4 fusion.169
  263.7 1.9 fusion.12
  265.6 3.2 fusion.36
  269.4 9.2 %fusion.6 = f32[64,8,32,2]{0,2,3,1:T(8,128)S(1)} fusion(bf16[8,32,2,8192]{3,2,1,0:T(2,128)(2,1)} %dot_general.201, f32[64]{0:T(128)S(1)} %get-tuple-element.125, f32[8192]{0:T(1024)S(1)} %copy-done.49, bf16[3,64,8192]{2,1,0:T(8,128)(2,1)S(1)} %copy-done.4), kind=kOutput, calls=%fused_computation.6 | convolution fusion | flops 538968064 | bytes 9601536 | tf_op jit(solution)/shard_map/dot_general | solution.py:161
  281.8 2.3 fusion.85
  286.9 2.2 fusion.99
  290.6 9.0 %fusion.8 = f32[64,8,32,2]{0,2,3,1:T(8,128)S(1)} fusion(bf16[8,32,2,8192]{3,2,1,0:T(2,128)(2,1)} %dot_general.201, f32[64]{0:T(128)} %get-tuple-element.126, f32[8192]{0:T(1024)} %param.19, bf16[3,64,8192]{2,1,0:T(8,128)(2,1)S(1)} %copy-done.4), kind=kOutput, calls=%fused_computation.8 | convolution fusion | flops 538968064 | bytes 9601280 | tf_op jit(solution)/shard_map/dot_general | solution.py:161
  305.1 1.9 pad_maximum_fusion.1
  306.9 2.7 copy.333
  310.9 9.0 %fusion.10 = f32[64,8,32,2]{0,2,3,1:T(8,128)S(1)} fusion(bf16[8,32,2,8192]{3,2,1,0:T(2,128)(2,1)} %dot_general.201, f32[8192]{0:T(1024)} %param.19, f32[64]{0:T(128)} %copy-done.52, bf16[3,64,8192]{2,1,0:T(8,128)(2,1)S(1)} %copy-done.4), kind=kOutput, calls=%fused_computation.10 | convolution fusion | flops 538968064 | bytes 9601280 | tf_op jit(solution)/shard_map/dot_general | solution.py:161
  320.9 2.4 fusion.105
  323.3 1.9 copy.281
  326.6 1.9 pad_maximum_fusion.3
  328.5 2.2 copy.282
  333.4 1.9 pad_maximum_fusion.2
  335.2 2.2 copy.311
  343.4 2.4 collective-permute-done
  345.8 2.2 copy.283
  350.1 5.3 collective-permute-done.1
  355.3 2.2 copy.312
  359.6 2.2 copy.334
  368.6 2.6 divide_convert_fusion.1
  378.6 2.6 fusion.65
  382.2 6.5 fusion.270
  388.7 6.3 fusion.268
  399.1 6.2 fusion.272
  405.4 268.8 %all-reduce.10.cloned.1.call-done = (f32[64,8192]{1,0:T(8,128)}, f32[64,8192]{1,0:T(8,128)}, f32[64,8192]{1,0:T(8,128)}, f32[64,4096]{1,0:T(8,128)}, f32[64,4096]{1,0:T(8,128)}) async-done(((f32[64,8192]{1,0:T(8,128)}, f32[64,8192]{1,0:T(8,128)}, f32[64,8192]{1,0:T(8,128)}, f32[64,4096]{1,0:T(8,128)}, f32[64,4096]{1,0:T(8,128)}), (f32[64,8192]{1,0:T(8,128)}, f32[64,8192]{1,0:T(8,128)}, ...) | async-done | bytes 8388624 | tf_op jit(solution)/shard_map/psum | solution.py:194
  674.9 13.3 %fusion.51 = f32[1,64,2,1024]{3,1,0,2:T(8,128)} fusion(bf16[1,2,1024,4096]{3,2,1,0:T(8,128)(2,1)} %param.31, f32[64,4096]{1,0:T(8,128)} %all-reduce.8.cloned.1.call-done, f32[4096]{0:T(1024)S(1)} %bitcast.557, f32[64]{0:T(128)S(1)} %add_rsqrt_fusion.8, bf16[1,3,64,4096]{3,2,1,0:T(8,128)(2,1)} %all-gather.6.cloned.1.call-done), kind=kOutput, calls=%fused_computation.72 | convolution fusion | flops 1075052544 | bytes 18891008 | tf_op jit(solution)/shard_map/dot_general | solution.py:153
  688.2 4.4 all-to-all-start
  692.7 2.3 multiply_reduce_fusion.4
  695.0 15.0 %fusion.54 = f32[1,64,2,1024]{3,1,0,2:T(8,128)} fusion(bf16[1,2,1024,4096]{3,2,1,0:T(8,128)(2,1)} %param.31, f32[64,4096]{1,0:T(8,128)} %get-tuple-element.39, f32[64]{0:T(128)S(1)} %add_rsqrt_fusion.4, f32[4096]{0:T(1024)S(1)} %bitcast.558, bf16[1,3,64,4096]{3,2,1,0:T(8,128)(2,1)} %all-gather.6.cloned.1.call-done), kind=kOutput, calls=%fused_computation.73 | convolution fusion | flops 1075052544 | bytes 18891008 | tf_op jit(solution)/shard_map/dot_general | solution.py:153
  710.0 12.3 %fusion.57 = f32[1,64,2,1024]{3,1,0,2:T(8,128)} fusion(bf16[1,2,1024,4096]{3,2,1,0:T(8,128)(2,1)} %param.31, f32[64,4096]{1,0:T(8,128)} %get-tuple-element.38, f32[64]{0:T(128)S(1)} %add_rsqrt_fusion, f32[4096]{0:T(1024)S(1)} %bitcast.559, bf16[1,3,64,4096]{3,2,1,0:T(8,128)(2,1)} %all-gather.6.cloned.1.call-done), kind=kOutput, calls=%fused_computation.74 | convolution fusion | flops 1075052544 | bytes 18891008 | tf_op jit(solution)/shard_map/dot_general | solution.py:153
  722.3 3.9 multiply_reduce_fusion.2
  726.2 4.5 all-to-all-start.1
  730.7 11.7 %fusion.267 = (f32[64]{0:T(128)S(1)}, f32[64,1024]{1,0:T(8,128)S(1)}) fusion(f32[2,1,64,1,1024]{4,2,3,1,0:T(8,128)} %bitcast.52, bf16[1024,8192]{1,0:T(8,128)(2,1)} %param.25, f32[64,8192]{1,0:T(8,128)} %get-tuple-element.41, f32[8192]{0:T(1024)S(1)} %copy-done.16, f32[64]{0:T(128)S(1)} %add_rsqrt_fusion.10, bf16[3,64,8192]{2,1,0:T(8,128)(2,1)S(1)} %copy-done.4), kind=kOutput, calls=%fused_computation.424 | convolution fusion | flops 1076559872 | bytes 20742912 | tf_op jit(solution)/shard_map/dot_general | solution.py:197
  742.4 4.2 all-to-all-start.2
  746.6 12.4 %fusion.266 = (f32[64]{0:T(128)S(1)}, f32[64,1024]{1,0:T(8,128)}) fusion(f32[2,1,64,1,1024]{4,2,3,1,0:T(8,128)} %bitcast.92, bf16[1024,8192]{1,0:T(8,128)(2,1)} %param.25, f32[64,8192]{1,0:T(8,128)} %get-tuple-element.42, f32[64]{0:T(128)S(1)} %add_rsqrt_fusion.6, f32[8192]{0:T(1024)S(1)} %copy-done.16, bf16[3,64,8192]{2,1,0:T(8,128)(2,1)S(1)} %copy-done.4), kind=kOutput, calls=%fused_computation.423 | convolution fusion | flops 1076559872 | bytes 20742912 | tf_op jit(solution)/shard_map/dot_general | solution.py:197
  759.1 12.4 %fusion.265 = (f32[64]{0:T(128)S(1)}, f32[64,1024]{1,0:T(8,128)}) fusion(f32[2,1,64,1,1024]{4,2,3,1,0:T(8,128)} %bitcast.128, bf16[1024,8192]{1,0:T(8,128)(2,1)} %param.25, f32[64,8192]{1,0:T(8,128)} %get-tuple-element.40, f32[64]{0:T(128)S(1)} %add_rsqrt_fusion.2, f32[8192]{0:T(1024)S(1)} %copy-done.16, bf16[3,64,8192]{2,1,0:T(8,128)(2,1)S(1)} %copy-done.4), kind=kOutput, calls=%fused_computation.422 | convolution fusion | flops 1076559872 | bytes 20742912 | tf_op jit(solution)/shard_map/dot_general | solution.py:197
  771.5 30.9 %all-reduce.1 = (f32[64]{0:T(128)S(1)}, f32[64]{0:T(128)S(1)}, f32[64]{0:T(128)S(1)}) all-reduce(f32[64]{0:T(128)S(1)} %get-tuple-element.119, f32[64]{0:T(128)S(1)} %get-tuple-element.121, f32[64]{0:T(128)S(1)} %get-tuple-element.123), channel_id=1, replica_groups=mesh['grp'=2,'tp'=8,'dp'=2] {'grp','tp'}, use_global_device_ids=true, to_apply=%region_50.51 | all-reduce | flops 192 | bytes 1536 | tf_op jit(solution)/shard_map/pmax | solution.py:205
  805.1 30.8 %all-reduce = (f32[64]{0:T(128)S(1)}, f32[64]{0:T(128)S(1)}, f32[64]{0:T(128)S(1)}, f32[64]{0:T(128)S(1)}, f32[64]{0:T(128)S(1)}, /*index=5*/f32[64]{0:T(128)S(1)}) all-reduce(f32[64]{0:T(128)S(1)} %get-tuple-element.18, f32[64]{0:T(128)S(1)} %get-tuple-element.16, ...), channel_id=1, replica_groups=mesh['grp'=2,'tp'=8,'dp'=2] {'grp','tp'}, use_global_device_ids=true, to_apply=%region_52.53 | all-reduce | flops 384 | bytes 3072 | tf_op jit(solution)/shard_map/psum | solution.py:206
  (286 shorter events, 73.6 us)
Async XLA Ops:
  8.0 57.4 %all-gather.6.cloned.1.call-start = ((), (), s32[]{:S(2)}) async-start(), calls=%async_computation.5 | async-start | bytes 1769472 | tf_op jit(solution)/shard_map/all_gather | solution.py:93
  8.7 195.0 %all-reduce.8.cloned.1.call-start = ((), (), s32[]{:S(2)}) async-start(), calls=%async_computation.4 | async-start | bytes 2097152 | tf_op jit(solution)/shard_map/psum | solution.py:150
  38.2 7.6 copy-start.41
  52.4 59.9 %copy-start.33 = (f32[64]{0:T(128)}, f32[64]{0:T(128)S(1)}, u32[]{:S(2)}) copy-start(f32[64]{0:T(128)S(1)} %get-tuple-element.112) | copy-start | bytes 772
  52.4 59.9 %copy-start.35 = (f32[64]{0:T(128)}, f32[64]{0:T(128)S(1)}, u32[]{:S(2)}) copy-start(f32[64]{0:T(128)S(1)} %get-tuple-element.113) | copy-start | bytes 772
  52.4 59.9 %copy-start.37 = (f32[64]{0:T(128)}, f32[64]{0:T(128)S(1)}, u32[]{:S(2)}) copy-start(f32[64]{0:T(128)S(1)} %get-tuple-element.114) | copy-start | bytes 772
  53.4 13.3 %copy-start.17 = (f32[1,4096]{1,0:T(1,128)S(1)}, f32[1,4096]{1,0:T(1,128)}, u32[]{:S(2)}) copy-start(f32[1,4096]{1,0:T(1,128)} %param.26) | copy-start | bytes 49156
  66.7 7.6 copy-start.5
  88.0 19.6 %copy-start = (bf16[512,4096]{1,0:T(8,128)(2,1)S(1)}, bf16[512,4096]{1,0:T(8,128)(2,1)}, u32[]{:S(2)}) copy-start(bf16[512,4096]{1,0:T(8,128)(2,1)} %copy.297) | copy-start | bytes 12582916
  107.5 2.2 copy-start.2
  111.7 154.0 %all-gather.4.cloned.1.call-start = ((), (), s32[]{:S(2)}) async-start(), calls=%async_computation.3 | async-start | bytes 3342336 | tf_op jit(solution)/shard_map/all_gather | solution.py:92
  112.2 561.9 %all-reduce.10.cloned.1.call-start = ((), (), s32[]{:S(2)}) async-start(), calls=%async_computation.6 | async-start | bytes 16777216 | tf_op jit(solution)/shard_map/psum | solution.py:194
  112.3 12.3 %copy-start.39 = (f32[32]{0:T(128)}, f32[32]{0:T(128)S(1)}, u32[]{:S(2)}) copy-start(f32[32]{0:T(128)S(1)} %multiply_exponential_fusion.1) | copy-start | bytes 388
  206.0 7.3 copy-start.11
  213.2 5.1 copy-start.21
  213.2 5.1 copy-start.22
  219.0 6.2 copy-start.10
  225.2 5.1 copy-start.12
  230.3 5.1 copy-start.20
  243.1 3.8 copy-start.1
  246.9 10.5 %slice-start = ((s8[8388608]{0:T(1024)(128)(4,1)}), s8[4194304]{0:T(1024)(128)(4,1)S(1)}, s32[]{:S(2)}) async-start(s8[8388608]{0:T(1024)(128)(4,1)} %bitcast.520), calls=%async_computation.8 | async-start | bytes 8388608
  249.0 8.4 slice-start.1
  257.4 4.5 copy-start.3
  263.7 5.7 copy-start.49
  265.6 3.8 copy-start.4
  269.4 9.2 %copy-start.44 = (f32[64]{0:T(128)}, f32[64]{0:T(128)S(1)}, u32[]{:S(2)}) copy-start(f32[64]{0:T(128)S(1)} %get-tuple-element.125) | copy-start | bytes 772
  269.4 9.2 %copy-start.28 = (f32[64,32]{0,1:T(8,128)S(1)}, f32[64,32]{0,1:T(8,128)}, u32[]{:S(2)}) copy-start(f32[64,32]{0,1:T(8,128)} %get-tuple-element.110) | copy-start | bytes 24580
  269.4 9.2 %copy-start.29 = (f32[64,32]{0,1:T(8,128)S(1)}, f32[64,32]{0,1:T(8,128)}, u32[]{:S(2)}) copy-start(f32[64,32]{0,1:T(8,128)} %get-tuple-element.111) | copy-start | bytes 24580
  279.0 6.1 copy-start.15
  281.8 2.4 copy-start.13
  281.8 2.4 copy-start.46
  281.8 2.4 copy-start.50
  281.8 3.4 copy-start.36
  281.8 3.4 copy-start.38
  281.8 3.4 copy-start.40
  281.8 5.1 copy-start.43
  284.2 4.9 copy-start.34
  286.9 2.4 copy-start.52
  290.6 9.0 %copy-start.26 = (f32[64,32]{0,1:T(8,128)S(1)}, f32[64,32]{0,1:T(8,128)}, u32[]{:S(2)}) copy-start(f32[64,32]{0,1:T(8,128)} %get-tuple-element.108) | copy-start | bytes 24580
  290.6 9.0 %copy-start.27 = (f32[64,32]{0,1:T(8,128)S(1)}, f32[64,32]{0,1:T(8,128)}, u32[]{:S(2)}) copy-start(f32[64,32]{0,1:T(8,128)} %get-tuple-element.109) | copy-start | bytes 24580
  309.6 10.3 %copy-start.24 = (f32[64,32]{0,1:T(8,128)S(1)}, f32[64,32]{0,1:T(8,128)}, u32[]{:S(2)}) copy-start(f32[64,32]{0,1:T(8,128)} %get-tuple-element.98) | copy-start | bytes 24580
  309.6 10.3 %copy-start.25 = (f32[64,32]{0,1:T(8,128)S(1)}, f32[64,32]{0,1:T(8,128)}, u32[]{:S(2)}) copy-start(f32[64,32]{0,1:T(8,128)} %get-tuple-element.99) | copy-start | bytes 24580
  309.6 50.0 %collective-permute-start.2 = (f32[64,8,131]{2,1,0:T(8,128)}, f32[64,8,131]{2,1,0:T(8,128)}, u32[]{:S(2)}, u32[]{:S(2)}) collective-permute-start(f32[64,8,131]{2,1,0:T(8,128)} %copy.333), channel_id=1, source_target_pairs={{0,2},{2,0},{4,6},{6,4},{8,10},{10,8},{12,14},{14,12},{1,3},{3,1},... | collective-permute-start | bytes 804872 | tf_op jit(solution)/shard_map/ppermute | solution.py:15
  326.0 12.7 %copy-start.47 = (f32[64]{0:T(128)S(1)}, f32[64]{0:T(128)}, u32[]{:S(2)}) copy-start(f32[64]{0:T(128)} %get-tuple-element.126) | copy-start | bytes 772
  326.1 12.7 %copy-start.51 = (f32[8192]{0:T(1024)S(1)}, f32[8192]{0:T(1024)}, u32[]{:S(2)}) copy-start(f32[8192]{0:T(1024)} %param.19) | copy-start | bytes 98308
  330.7 15.1 %collective-permute-start = (f32[64,8,129]{2,1,0:T(8,128)}, f32[64,8,129]{2,1,0:T(8,128)}, u32[]{:S(2)}, u32[]{:S(2)}) collective-permute-start(f32[64,8,129]{2,1,0:T(8,128)} %copy.282), channel_id=1, source_target_pairs={{0,2},{2,0},{4,6},{6,4},{8,10},{10,8},{12,14},{14,12},{1,3},{3,1},... | collective-permute-start | bytes 792584 | tf_op jit(solution)/shard_map/ppermute | solution.py:15
  332.3 8.2 copy-start.53
  337.4 3.0 copy-start.14
  337.5 4.2 copy-start.45
  337.5 17.9 %collective-permute-start.1 = (f32[64,8,130]{2,1,0:T(8,128)}, f32[64,8,130]{2,1,0:T(8,128)}, u32[]{:S(2)}, u32[]{:S(2)}) collective-permute-start(f32[64,8,130]{2,1,0:T(8,128)} %copy.311), channel_id=1, source_target_pairs={{0,2},{2,0},{4,6},{6,4},{8,10},{10,8},{12,14},{14,12},{1,3},{3,1},... | collective-permute-start | bytes 798728 | tf_op jit(solution)/shard_map/ppermute | solution.py:15
  341.6 6.4 copy-start.31
  348.0 13.8 %copy-start.23 = (f32[64,8,3]{0,1,2:T(8,128)S(1)}, f32[64,8,3]{0,1,2:T(8,128)}, u32[]{:S(2)}) copy-start(f32[64,8,3]{0,1,2:T(8,128)} %copy.332) | copy-start | bytes 18436
  349.3 0.8 copy-start.9
  358.8 0.8 copy-start.7
  361.8 3.1 copy-start.8
  363.1 2.1 copy-start.6
  388.7 6.3 copy-start.32
  405.4 316.9 %all-reduce.12.cloned.1.call-start = ((), (), s32[]{:S(2)}) async-start(), calls=%async_computation.7 | async-start | bytes 12582912 | tf_op jit(solution)/shard_map/psum | solution.py:194
  674.2 0.7 copy-start.48
  674.2 0.7 copy-start.18
  688.2 37.9 %all-to-all-start = ((f32[1,64,2,1024]{3,1,0,2:T(8,128)}), f32[1,64,2,1024]{3,1,0,2:T(8,128)}, u32[]{:S(2)}, u32[]{:S(2)}) async-start(f32[1,64,2,1024]{3,1,0,2:T(8,128)} %fusion.51), calls=%async_computation | async-start | bytes 1048576 | tf_op jit(solution)/shard_map/all_to_all | solution.py:157
  722.3 8.4 copy-start.16
  726.2 16.2 %all-to-all-start.1 = ((f32[1,64,2,1024]{3,1,0,2:T(8,128)}), f32[1,64,2,1024]{3,1,0,2:T(8,128)}, u32[]{:S(2)}, u32[]{:S(2)}) async-start(f32[1,64,2,1024]{3,1,0,2:T(8,128)} %fusion.54), calls=%async_computation.1 | async-start | bytes 1048576 | tf_op jit(solution)/shard_map/all_to_all | solution.py:157
  742.4 16.7 %all-to-all-start.2 = ((f32[1,64,2,1024]{3,1,0,2:T(8,128)}), f32[1,64,2,1024]{3,1,0,2:T(8,128)}, u32[]{:S(2)}, u32[]{:S(2)}) async-start(f32[1,64,2,1024]{3,1,0,2:T(8,128)} %fusion.57), calls=%async_computation.2 | async-start | bytes 1048576 | tf_op jit(solution)/shard_map/all_to_all | solution.py:157
  (3 other events, 1.9 us)
Sparse Core Ops, SparseCore 0:
  10.8 47.1 all-gather.5
  111.8 91.8 all-reduce.7
  405.5 268.6 all-reduce.9
Sparse Core Ops, SparseCore 1:
  114.2 52.9 all-gather.3
  674.3 30.9 all-reduce.11
